TPU v7x, 32 devices: a whole 2x2x4 slice. The times are simulated.
32 devices in a mesh: sweep: 4 (over z), cross: 2 (over y), third: 4 (over x, core).
Axes of the slice: x: 2, y: 2, z: 4, core: 2. Of those that a mesh axis runs over, the one named last changes fastest.
Arguments:
- rhs: float32 [32, 32, 64, 128], P('sweep', 'cross', 'third'), may hold values from -6 to 6
- guess: float32 [32, 32, 64, 128], P('sweep', 'cross', 'third'), may hold values from -6 to 6
- inv_diag: float32 [128, 128], replicated, may hold values from -0.25 to 1.25
- face_mats: float32 [6, 32, 128], replicated, may hold values from -0.4375 to 0.4375
- extract: float32 [4, 128, 32], replicated, may hold values from -0.5 to 0.5
- lift: float32 [32, 96], replicated, may hold values from -1 to 1
- transport: float32 [32, 32], P('sweep'), may hold values from 0 to 1, as said below
- boundary: float32 [32, 64, 32], P('cross', 'third'), may hold values from -6 to 6
- scale_index: int32 [32, 32, 64], P('sweep', 'cross', 'third'), may hold values from 0 to 3
- wind: int32 [2, 32, 32, 64], P(None, 'sweep', 'cross', 'third'), may hold values from 0 to 1
Outputs:
- solution: float32 [32, 32, 64, 128], P('sweep', 'cross', 'third')
Inputs may be any that keep to these rules, and one draw needn't show every extreme that they name: `transport`: transmission factors are positive.
All inputs are finite; a program needn't handle non-finite values.
Results may differ from a plain program's by a relative error of at most 0.0003.
Values sent between devices are 32-bit elements; how exact they have to be, the bound alone decides.
A program may use at most 64 MiB of HBM per device.

v0:
```python
import jax
import jax.numpy as jnp
from jax import lax
from jax.sharding import PartitionSpec as P

SWEEPS = 2


def padded_2(cells, sides, width):
    for axis, dim in sides:
        count = lax.axis_size(axis)
        ends = count - 1
        head = lax.slice_in_dim(cells, 0, width, axis=dim)
        tail = lax.slice_in_dim(cells, cells.shape[dim] - width, cells.shape[dim], axis=dim)
        cells = jnp.concatenate(
            [
                lax.ppermute(tail, axis, [(i, (i + 1) % count) for i in range(ends)]),
                cells,
                lax.ppermute(head, axis, [((i + 1) % count, i) for i in range(ends)]),
            ],
            axis=dim,
        )
    return cells


def passed_along(value, axis, steps):
    count = lax.axis_size(axis)
    first, last = (max(0, -steps), min(count, count - steps))
    return lax.ppermute(value, axis, [(source, source + steps) for source in range(first, last)])


def product(left, right):
    return jnp.einsum(
        "...i,ij->...j",
        left,
        right,
        precision=lax.Precision.HIGHEST,
        preferred_element_type=jnp.float32,
    )


def neighbour_traces(field, extract):
    padded = padded_2(field, (("cross", 1), ("third", 2)), 1)
    low_y = product(padded[:, :-2, 1:-1], extract[0])
    high_y = product(padded[:, 2:, 1:-1], extract[1])
    low_z = product(padded[:, 1:-1, :-2], extract[2])
    high_z = product(padded[:, 1:-1, 2:], extract[3])
    return (low_y, high_y, low_z, high_z)


def chain_inflow(gain, total, boundary):
    first = lax.axis_index("sweep") == 0

    def relay_step(count, current):
        leaving = gain * current + total
        arrived = passed_along(leaving, "sweep", 1)
        return jnp.where(first, boundary, arrived)

    return lax.fori_loop(0, lax.axis_size("sweep") - 1, relay_step, boundary)


def sweep_once(
    field, rhs, inv_diag, faces_flat, extract, lift, transmit, diffusion, wind, boundary
):
    low_y, high_y, low_z, high_z = neighbour_traces(field, extract)
    scaled = diffusion[..., None]
    pick_y = jnp.where(wind[0][..., None] == 1, low_y, high_y)
    pick_z = jnp.where(wind[1][..., None] == 1, low_z, high_z)
    stacked = jnp.concatenate(
        [scaled * low_y, scaled * high_y, pick_y, scaled * low_z, scaled * high_z, pick_z], axis=-1
    )
    lateral = product(stacked, faces_flat)
    base = product(rhs - lateral, inv_diag) / (1.0 + scaled)
    width = transmit.shape[-1]
    inner = base.shape[-1] - width
    outflow = base[..., inner:]
    carry_gain = jnp.ones_like(outflow[0])
    carry_sum = jnp.zeros_like(outflow[0])
    gains = []
    sums = []
    for position in range(base.shape[0]):
        gains.append(carry_gain)
        sums.append(carry_sum)
        carry_sum = transmit[position] * carry_sum + outflow[position]
        carry_gain = transmit[position] * carry_gain
    incoming = chain_inflow(carry_gain, carry_sum, boundary)
    inflow = jnp.stack(gains) * incoming[None] + jnp.stack(sums)
    leaving = transmit * inflow + outflow
    return jnp.concatenate([base[..., :inner] + product(inflow, lift), leaving], axis=-1)


def per_device(
    rhs, guess, inv_diag, face_mats, extract, lift, transport, boundary, scale_index, wind
):
    diffusion = 0.5 + 0.25 * scale_index.astype(jnp.float32)
    transmit = jnp.exp(diffusion[..., None] * jnp.log(transport)[:, None, None, :])
    faces_flat = face_mats.reshape(-1, face_mats.shape[2])
    field = guess
    for repeat in range(SWEEPS):
        field = sweep_once(
            field, rhs, inv_diag, faces_flat, extract, lift, transmit, diffusion, wind, boundary
        )
    return field


def solution(mesh):
    return jax.shard_map(
        per_device,
        mesh=mesh,
        in_specs=(
            P("sweep", "cross", "third", None),
            P("sweep", "cross", "third", None),
            P(),
            P(),
            P(),
            P(),
            P("sweep", None),
            P("cross", "third", None),
            P("sweep", "cross", "third"),
            P(None, "sweep", "cross", "third"),
        ),
        out_specs=P("sweep", "cross", "third", None),
        check_vma=False,
    )
```

profile of v0, /device:TPU:25, one launch (start us, length us, event | category | flops | bytes accessed | tf_op | source)
XLA Modules:
  0.0 141.7 jit_solution(12213023303991248673)
XLA Ops:
  2.3 4.0 %collective-permute-start.2 = (f32[8,1,16,128]{3,2,1,0:T(8,128)S(1)}, f32[8,1,16,128]{3,2,1,0:T(8,128)S(1)}, u32[]{:S(2)}, u32[]{:S(2)}) collective-permute-start(f32[8,1,16,128]{3,2,1,0:T(8,128)S(1)} %get-tuple-element.130), channel_id=1, source_target_pairs={{0,4},{1,5},{2,6},{3,7},{8,12},{9,13},{10,14},{11,15},{16,20},{17,... | collective-permute-start | bytes 196616 | tf_op jit(solution)/shard_map/ppermute | solution.py:17
  7.9 1.6 %copy.48 = f32[16,16,32]{2,1,0:T(8,128)} copy(f32[16,16,32]{2,1,0:T(8,128)} %param.21) | data formatting | bytes 65536
  13.6 2.3 %broadcast_select_fusion.5 = (f32[8,16,16,32]{3,2,1,0:T(8,128)}, f32[8,16,16,32]{3,2,1,0:T(8,128)}, f32[8,16,16,32]{3,2,1,0:T(8,128)}, f32[8,16,16,32]{3,2,1,0:T(8,128)S(1)}) fusion(f32[8,16,16,32]{3,2,1,0:T(8,128)S(1)} %fusion.4, pred[8,16,16]{2,1,0:T(8,128)(4,1)S(1)} %get-tuple-element.132, f32[8,16,16]{2,1,0:T(8,128)S(1)} %get-tuple-element.135, ...), kind=kOutput, calls=%fused_computation.65 | convolution fusion | flops 101203968 | bytes 3313664 | tf_op jit(solution)/shard_map/...i,ij->...j/dot_general | solution.py:33
  16.8 3.1 %collective-permute-start.5 = (f32[8,18,1,128]{3,2,1,0:T(1,128)S(1)}, f32[8,18,1,128]{3,2,1,0:T(1,128)S(1)}, u32[]{:S(2)}, u32[]{:S(2)}) collective-permute-start(f32[8,18,1,128]{3,2,1,0:T(1,128)S(1)} %get-tuple-element.113), channel_id=1, source_target_pairs={{1,0},{2,1},{3,2},{5,4},{6,5},{7,6},{9,8},{10,9},{11,10},{13,12},{... | collective-permute-start | bytes 221192 | tf_op jit(solution)/shard_map/ppermute | solution.py:19
  20.1 3.0 %collective-permute-start.4 = (f32[8,18,1,128]{3,2,1,0:T(1,128)S(1)}, f32[8,18,1,128]{3,2,1,0:T(1,128)S(1)}, u32[]{:S(2)}, u32[]{:S(2)}) collective-permute-start(f32[8,18,1,128]{3,2,1,0:T(1,128)S(1)} %get-tuple-element.114), channel_id=1, source_target_pairs={{0,1},{1,2},{2,3},{4,5},{5,6},{6,7},{8,9},{9,10},{10,11},{12,13},{... | collective-permute-start | bytes 221192 | tf_op jit(solution)/shard_map/ppermute | solution.py:17
  24.5 2.3 %broadcast_select_fusion.3 = (f32[8,16,16,32]{3,2,1,0:T(8,128)}, f32[8,16,16,32]{3,2,1,0:T(8,128)}, f32[8,16,16,32]{3,2,1,0:T(8,128)}) fusion(f32[8,16,16,32]{3,2,1,0:T(8,128)S(1)} %fusion.24, pred[8,16,16]{2,1,0:T(8,128)(4,1)S(1)} %get-tuple-element.131, f32[8,16,16]{2,1,0:T(8,128)S(1)} %get-tuple-element.135, f32[4,128,32]{1,2,0:T(8,128)S(1)} %copy-done.15, ...), kind=kOutput, calls=%fused_computation.63 | convolution fusion | flops 101122048 | bytes 3186688 | tf_op jit(solution)/shard_map/...i,ij->...j/dot_general | solution.py:33
  26.8 5.2 %concatenate.49 = f32[8,16,16,192]{3,2,1,0:T(8,128)} concatenate(f32[8,16,16,32]{3,2,1,0:T(8,128)} %get-tuple-element.128, f32[8,16,16,32]{3,2,1,0:T(8,128)} %get-tuple-element.127, f32[8,16,16,32]{3,2,1,0:T(8,128)} %get-tuple-element.126, f32[8,16,16,32]{3,2,1,0:T(8,128)} %get-tuple-element.125, f32[8,16,16,32]{3,2,1,0:T(8,128)} %get-tuple-element.124, ...), dimensions={3} | concatenate | bytes 3145728 | tf_op jit(solution)/shard_map/concatenate | solution.py:69
  32.1 3.5 %convolution_subtract_fusion.1 = f32[8,16,16,128]{3,2,1,0:T(8,128)S(1)} fusion(f32[8,16,16,128]{3,2,1,0:T(8,128)S(1)} %copy-done.8, f32[8,16,16,192]{3,2,1,0:T(8,128)} %concatenate.49, f32[192,128,1,1]{1,0,3,2:T(8,128)S(1)} %bitcast.216), kind=kOutput, calls=%fused_computation.9 | convolution fusion | flops 604241920 | bytes 3768320 | tf_op jit(solution)/shard_map/...i,ij->...j/dot_general | solution.py:33
  43.0 29.7 %while.20 = (s32[]{:T(128)}, f32[16,16,32]{2,1,0:T(8,128)}, pred[]{:T(512)}, f32[16,16,32]{2,1,0:T(8,128)S(1)}, f32[16,16,32]{2,1,0:T(8,128)}, /*index=5*/f32[16,16,32]{2,1,0:T(8,128)S(1)}, s32[]{:T(128)}) while((s32[]{:T(128)}, f32[16,16,32]{2,1,0:T(8,128)}, pred[]{:T(512)}, f32[16,16,32]{2,1,0:T(8,128)S(1)}, f32[16,16,32]{2,1,0:T(8,128)}, ...), condition=%wide.region_1.2_spmd, body=%wide.region_0.1_spmd.sunk | while | flops 24578 | bytes 360566 | solution.py:59
  43.0 1.6 %multiply_add_fusion.24 = f32[16,16,32]{2,1,0:T(8,128)} fusion(f32[16,16,32]{2,1,0:T(8,128)} %get-tuple-element.228, f32[16,16,32]{2,1,0:T(8,128)S(1)} %get-tuple-element.227, f32[16,16,32]{2,1,0:T(8,128)} %get-tuple-element.218), kind=kLoop, calls=%fused_computation.clone.1 | loop fusion | flops 16384 | bytes 131072 | tf_op jit(solution)/shard_map/while/body/eval_jaxpr/add | solution.py:55
  45.9 5.7 %collective-permute-done = f32[16,16,32]{2,1,0:T(8,128)} collective-permute-done((f32[16,16,32]{2,1,0:T(8,128)}, f32[16,16,32]{2,1,0:T(8,128)}, u32[]{:S(2)}, u32[]{:S(2)}) %collective-permute-start) | collective-permute-done | bytes 32800 | tf_op jit(solution)/shard_map/while/body/eval_jaxpr/ppermute | solution.py:29
  51.5 1.6 %broadcast_select_fusion.8 = f32[16,16,32]{2,1,0:T(8,128)} fusion(f32[16,16,32]{2,1,0:T(8,128)S(1)} %get-tuple-element.229, f32[16,16,32]{2,1,0:T(8,128)} %collective-permute-done, pred[]{:T(512)} %get-tuple-element.226), kind=kLoop, calls=%fused_computation.1.clone.1 | loop fusion | flops 8192 | bytes 98305 | tf_op jit(solution)/shard_map/while/body/eval_jaxpr/jit(_where)/select_n | solution.py:57
  53.1 1.6 %multiply_add_fusion.24 = f32[16,16,32]{2,1,0:T(8,128)} fusion(f32[16,16,32]{2,1,0:T(8,128)} %get-tuple-element.228, f32[16,16,32]{2,1,0:T(8,128)S(1)} %get-tuple-element.227, f32[16,16,32]{2,1,0:T(8,128)} %get-tuple-element.218), kind=kLoop, calls=%fused_computation.clone.1 | loop fusion | flops 16384 | bytes 131072 | tf_op jit(solution)/shard_map/while/body/eval_jaxpr/add | solution.py:55
  56.0 5.8 %collective-permute-done = f32[16,16,32]{2,1,0:T(8,128)} collective-permute-done((f32[16,16,32]{2,1,0:T(8,128)}, f32[16,16,32]{2,1,0:T(8,128)}, u32[]{:S(2)}, u32[]{:S(2)}) %collective-permute-start) | collective-permute-done | bytes 32800 | tf_op jit(solution)/shard_map/while/body/eval_jaxpr/ppermute | solution.py:29
  61.8 1.6 %broadcast_select_fusion.8 = f32[16,16,32]{2,1,0:T(8,128)} fusion(f32[16,16,32]{2,1,0:T(8,128)S(1)} %get-tuple-element.229, f32[16,16,32]{2,1,0:T(8,128)} %collective-permute-done, pred[]{:T(512)} %get-tuple-element.226), kind=kLoop, calls=%fused_computation.1.clone.1 | loop fusion | flops 8192 | bytes 98305 | tf_op jit(solution)/shard_map/while/body/eval_jaxpr/jit(_where)/select_n | solution.py:57
  63.4 1.6 %multiply_add_fusion.24 = f32[16,16,32]{2,1,0:T(8,128)} fusion(f32[16,16,32]{2,1,0:T(8,128)} %get-tuple-element.228, f32[16,16,32]{2,1,0:T(8,128)S(1)} %get-tuple-element.227, f32[16,16,32]{2,1,0:T(8,128)} %get-tuple-element.218), kind=kLoop, calls=%fused_computation.clone.1 | loop fusion | flops 16384 | bytes 131072 | tf_op jit(solution)/shard_map/while/body/eval_jaxpr/add | solution.py:55
  66.3 4.7 %collective-permute-done = f32[16,16,32]{2,1,0:T(8,128)} collective-permute-done((f32[16,16,32]{2,1,0:T(8,128)}, f32[16,16,32]{2,1,0:T(8,128)}, u32[]{:S(2)}, u32[]{:S(2)}) %collective-permute-start) | collective-permute-done | bytes 32800 | tf_op jit(solution)/shard_map/while/body/eval_jaxpr/ppermute | solution.py:29
  71.0 1.6 %broadcast_select_fusion.8 = f32[16,16,32]{2,1,0:T(8,128)} fusion(f32[16,16,32]{2,1,0:T(8,128)S(1)} %get-tuple-element.229, f32[16,16,32]{2,1,0:T(8,128)} %collective-permute-done, pred[]{:T(512)} %get-tuple-element.226), kind=kLoop, calls=%fused_computation.1.clone.1 | loop fusion | flops 8192 | bytes 98305 | tf_op jit(solution)/shard_map/while/body/eval_jaxpr/jit(_where)/select_n | solution.py:57
  72.6 1.9 %slice_add_fusion.1 = f32[8,16,16,32]{3,2,1,0:T(8,128)S(1)} fusion(f32[8,16,16,128]{3,2,1,0:T(8,128)S(1)} %convolution_divide_fusion.1, f32[8,32]{1,0:T(8,128)} %copy-done.20, f32[8,16,16]{2,1,0:T(8,128)} %copy-done.10, f32[8,16,16,32]{3,2,1,0:T(8,128)} %add_dynamic-update-slice_fusion.1, f32[8,16,16,32]{3,2,1,0:T(8,128)S(1)} %get-tuple-element.121, ...), kind=kLoop, calls=%fused_computation.43 | loop fusion | flops 327680 | bytes 1090560 | tf_op jit(solution)/shard_map/add | solution.py:88
  74.6 2.2 %convolution_add_fusion.1 = f32[8,16,16,96]{3,2,1,0:T(8,128)S(1)} fusion(f32[8,16,16,128]{3,2,1,0:T(8,128)S(1)} %convolution_divide_fusion.1, f32[8,16,16,32]{3,2,1,0:T(8,128)} %add_dynamic-update-slice_fusion.1, f32[8,16,16,32]{3,2,1,0:T(8,128)S(1)} %get-tuple-element.121, f32[16,16,32]{2,1,0:T(8,128)S(1)} %copy-done.4, f32[32,96]{1,0:T(8,128)S(1)} %copy-done.17), kind=kOutput, calls=%fused_computation.7 | convolution fusion | flops 75825152 | bytes 2142208 | tf_op jit(solution)/shard_map/...i,ij->...j/dot_general | solution.py:33
  80.2 3.0 %collective-permute-done.7 = f32[8,1,16,128]{3,2,1,0:T(8,128)S(1)} collective-permute-done((f32[8,1,16,128]{3,2,1,0:T(8,128)S(1)}, f32[8,1,16,128]{3,2,1,0:T(8,128)S(1)}, u32[]{:S(2)}, u32[]{:S(2)}) %collective-permute-start.7) | collective-permute-done | bytes 65568 | tf_op jit(solution)/shard_map/ppermute | solution.py:19
  83.6 5.3 %collective-permute-start.9 = (f32[8,18,1,128]{3,2,1,0:T(1,128)S(1)}, f32[8,18,1,128]{3,2,1,0:T(1,128)S(1)}, u32[]{:S(2)}, u32[]{:S(2)}) collective-permute-start(f32[8,18,1,128]{3,2,1,0:T(1,128)S(1)} %get-tuple-element.109), channel_id=1, source_target_pairs={{1,0},{2,1},{3,2},{5,4},{6,5},{7,6},{9,8},{10,9},{11,10},{13,12},{... | collective-permute-start | bytes 221192 | tf_op jit(solution)/shard_map/ppermute | solution.py:19
  88.9 3.9 %collective-permute-start.8 = (f32[8,18,1,128]{3,2,1,0:T(1,128)S(1)}, f32[8,18,1,128]{3,2,1,0:T(1,128)S(1)}, u32[]{:S(2)}, u32[]{:S(2)}) collective-permute-start(f32[8,18,1,128]{3,2,1,0:T(1,128)S(1)} %get-tuple-element.110), channel_id=1, source_target_pairs={{0,1},{1,2},{2,3},{4,5},{5,6},{6,7},{8,9},{9,10},{10,11},{12,13},{... | collective-permute-start | bytes 221192 | tf_op jit(solution)/shard_map/ppermute | solution.py:17
  93.8 2.4 %broadcast_select_fusion.4 = (f32[8,16,16,32]{3,2,1,0:T(8,128)}, f32[8,16,16,32]{3,2,1,0:T(8,128)}, f32[8,16,16,32]{3,2,1,0:T(8,128)}) fusion(f32[8,16,16,32]{3,2,1,0:T(8,128)S(1)} %fusion.14, pred[8,16,16]{2,1,0:T(8,128)(4,1)S(1)} %get-tuple-element.132, f32[8,16,16]{2,1,0:T(8,128)S(1)} %copy-done.11, f32[4,128,32]{1,2,0:T(8,128)S(1)} %copy-done.16, ...), kind=kOutput, calls=%fused_computation.64 | convolution fusion | flops 101416960 | bytes 4096000 | tf_op jit(solution)/shard_map/...i,ij->...j/dot_general | solution.py:33
  97.5 2.6 %broadcast_select_fusion.2 = (f32[8,16,16,32]{3,2,1,0:T(8,128)}, f32[8,16,16,32]{3,2,1,0:T(8,128)}, f32[8,16,16,32]{3,2,1,0:T(8,128)}) fusion(f32[8,16,16,32]{3,2,1,0:T(8,128)S(1)} %fusion.20, pred[8,16,16]{2,1,0:T(8,128)(4,1)S(1)} %get-tuple-element.131, f32[8,16,16]{2,1,0:T(8,128)S(1)} %copy-done.11, f32[4,128,32]{1,2,0:T(8,128)S(1)} %copy-done.16, ...), kind=kOutput, calls=%fused_computation.62 | convolution fusion | flops 101908480 | bytes 4235264 | tf_op jit(solution)/shard_map/...i,ij->...j/dot_general | solution.py:33
  100.1 5.2 %concatenate.56 = f32[8,16,16,192]{3,2,1,0:T(8,128)} concatenate(f32[8,16,16,32]{3,2,1,0:T(8,128)} %get-tuple-element.120, f32[8,16,16,32]{3,2,1,0:T(8,128)} %get-tuple-element.119, f32[8,16,16,32]{3,2,1,0:T(8,128)} %get-tuple-element.118, f32[8,16,16,32]{3,2,1,0:T(8,128)} %get-tuple-element.117, f32[8,16,16,32]{3,2,1,0:T(8,128)} %get-tuple-element.116, ...), dimensions={3} | concatenate | bytes 3145728 | tf_op jit(solution)/shard_map/concatenate | solution.py:69
  105.3 3.5 %convolution_subtract_fusion = f32[8,16,16,128]{3,2,1,0:T(8,128)S(1)} fusion(f32[8,16,16,128]{3,2,1,0:T(8,128)S(1)} %copy-done.9, f32[8,16,16,192]{3,2,1,0:T(8,128)} %concatenate.56, f32[192,128,1,1]{1,0,3,2:T(8,128)S(1)} %bitcast.217), kind=kOutput, calls=%fused_computation.6 | convolution fusion | flops 604241920 | bytes 3768320 | tf_op jit(solution)/shard_map/...i,ij->...j/dot_general | solution.py:33
  112.8 24.5 %while.21 = (s32[]{:T(128)}, f32[16,16,32]{2,1,0:T(8,128)}, pred[]{:T(512)}, f32[16,16,32]{2,1,0:T(8,128)S(1)}, f32[16,16,32]{2,1,0:T(8,128)}, /*index=5*/f32[16,16,32]{2,1,0:T(8,128)S(1)}, s32[]{:T(128)}) while((s32[]{:T(128)}, f32[16,16,32]{2,1,0:T(8,128)}, pred[]{:T(512)}, f32[16,16,32]{2,1,0:T(8,128)S(1)}, f32[16,16,32]{2,1,0:T(8,128)}, ...), condition=%wide.region_3.4_spmd, body=%wide.region_2.3_spmd.sunk | while | flops 24578 | bytes 360566 | solution.py:59
  115.1 5.1 %collective-permute-done.1 = f32[16,16,32]{2,1,0:T(8,128)S(1)} collective-permute-done((f32[16,16,32]{2,1,0:T(8,128)S(1)}, f32[16,16,32]{2,1,0:T(8,128)S(1)}, u32[]{:S(2)}, u32[]{:S(2)}) %collective-permute-start.1) | collective-permute-done | bytes 32800 | tf_op jit(solution)/shard_map/while/body/eval_jaxpr/ppermute | solution.py:29
  123.2 5.6 %collective-permute-done.1 = f32[16,16,32]{2,1,0:T(8,128)S(1)} collective-permute-done((f32[16,16,32]{2,1,0:T(8,128)S(1)}, f32[16,16,32]{2,1,0:T(8,128)S(1)}, u32[]{:S(2)}, u32[]{:S(2)}) %collective-permute-start.1) | collective-permute-done | bytes 32800 | tf_op jit(solution)/shard_map/while/body/eval_jaxpr/ppermute | solution.py:29
  131.9 4.8 %collective-permute-done.1 = f32[16,16,32]{2,1,0:T(8,128)S(1)} collective-permute-done((f32[16,16,32]{2,1,0:T(8,128)S(1)}, f32[16,16,32]{2,1,0:T(8,128)S(1)}, u32[]{:S(2)}, u32[]{:S(2)}) %collective-permute-start.1) | collective-permute-done | bytes 32800 | tf_op jit(solution)/shard_map/while/body/eval_jaxpr/ppermute | solution.py:29
  137.3 2.3 %convolution_add_fusion = f32[8,16,16,96]{3,2,1,0:T(8,128)S(1)} fusion(f32[8,16,16,128]{3,2,1,0:T(8,128)S(1)} %convolution_divide_fusion, f32[8,16,16,32]{3,2,1,0:T(8,128)} %copy-done.6, f32[8,16,16,32]{3,2,1,0:T(8,128)S(1)} %get-tuple-element.121, f32[16,16,32]{2,1,0:T(8,128)} %get-tuple-element.70, f32[32,96]{1,0:T(8,128)S(1)} %copy-done.17), kind=kOutput, calls=%fused_computation.4 | convolution fusion | flops 75825152 | bytes 2142208 | tf_op jit(solution)/shard_map/...i,ij->...j/dot_general | solution.py:33
  (117 shorter events, 42.3 us)
Async XLA Ops:
  0.0 32.0 %copy-start = (f32[6,32,128]{2,1,0:T(8,128)S(1)}, f32[6,32,128]{2,1,0:T(8,128)}, u32[]{:S(2)}) copy-start(f32[6,32,128]{2,1,0:T(8,128)} %param.17) | copy-start | bytes 294916
  0.0 12.6 %copy-start.2 = (f32[8,16,16,128]{3,2,1,0:T(8,128)S(1)}, f32[8,16,16,128]{3,2,1,0:T(8,128)}, u32[]{:S(2)}) copy-start(f32[8,16,16,128]{3,2,1,0:T(8,128)} %param.15) | copy-start | bytes 3145732
  0.0 11.8 %copy-start.22 = (f32[8,32]{1,0:T(8,128)S(1)}, f32[8,32]{1,0:T(8,128)}, u32[]{:S(2)}) copy-start(f32[8,32]{1,0:T(8,128)} %param.20) | copy-start | bytes 3076
  0.0 12.6 %copy-start.15 = (f32[4,128,32]{1,2,0:T(8,128)S(1)}, f32[4,128,32]{1,2,0:T(8,128)}, u32[]{:S(2)}) copy-start(f32[4,128,32]{1,2,0:T(8,128)} %param.18) | copy-start | bytes 196612
  1.0 11.5 %collective-permute-start.3 = (f32[8,1,16,128]{3,2,1,0:T(8,128)S(1)}, f32[8,1,16,128]{3,2,1,0:T(8,128)S(1)}, u32[]{:S(2)}, u32[]{:S(2)}) collective-permute-start(f32[8,1,16,128]{3,2,1,0:T(8,128)S(1)} %get-tuple-element.129), channel_id=1, source_target_pairs={{4,0},{5,1},{6,2},{7,3},{12,8},{13,9},{14,10},{15,11},{20,16},{21,... | collective-permute-start | bytes 196616 | tf_op jit(solution)/shard_map/ppermute | solution.py:19
  2.3 11.2 %collective-permute-start.2 = (f32[8,1,16,128]{3,2,1,0:T(8,128)S(1)}, f32[8,1,16,128]{3,2,1,0:T(8,128)S(1)}, u32[]{:S(2)}, u32[]{:S(2)}) collective-permute-start(f32[8,1,16,128]{3,2,1,0:T(8,128)S(1)} %get-tuple-element.130), channel_id=1, source_target_pairs={{0,4},{1,5},{2,6},{3,7},{8,12},{9,13},{10,14},{11,15},{16,20},{17,... | collective-permute-start | bytes 196616 | tf_op jit(solution)/shard_map/ppermute | solution.py:17
  10.9 13.6 %copy-start.10 = (f32[8,16,16]{2,1,0:T(8,128)}, f32[8,16,16]{2,1,0:T(8,128)S(1)}, u32[]{:S(2)}) copy-start(f32[8,16,16]{2,1,0:T(8,128)S(1)} %get-tuple-element.135) | copy-start | bytes 24580
  11.9 4.0 %copy-start.20 = (f32[8,32]{1,0:T(8,128)}, f32[8,32]{1,0:T(8,128)S(1)}, u32[]{:S(2)}) copy-start(f32[8,32]{1,0:T(8,128)S(1)} %log.3) | copy-start | bytes 3076
  16.8 6.3 %collective-permute-start.5 = (f32[8,18,1,128]{3,2,1,0:T(1,128)S(1)}, f32[8,18,1,128]{3,2,1,0:T(1,128)S(1)}, u32[]{:S(2)}, u32[]{:S(2)}) collective-permute-start(f32[8,18,1,128]{3,2,1,0:T(1,128)S(1)} %get-tuple-element.113), channel_id=1, source_target_pairs={{1,0},{2,1},{3,2},{5,4},{6,5},{7,6},{9,8},{10,9},{11,10},{13,12},{... | collective-permute-start | bytes 221192 | tf_op jit(solution)/shard_map/ppermute | solution.py:19
  20.1 4.4 %collective-permute-start.4 = (f32[8,18,1,128]{3,2,1,0:T(1,128)S(1)}, f32[8,18,1,128]{3,2,1,0:T(1,128)S(1)}, u32[]{:S(2)}, u32[]{:S(2)}) collective-permute-start(f32[8,18,1,128]{3,2,1,0:T(1,128)S(1)} %get-tuple-element.114), channel_id=1, source_target_pairs={{0,1},{1,2},{2,3},{4,5},{5,6},{6,7},{8,9},{9,10},{10,11},{12,13},{... | collective-permute-start | bytes 221192 | tf_op jit(solution)/shard_map/ppermute | solution.py:17
  26.8 5.2 %copy-start.8 = (f32[8,16,16,128]{3,2,1,0:T(8,128)S(1)}, f32[8,16,16,128]{3,2,1,0:T(8,128)}, u32[]{:S(2)}) copy-start(f32[8,16,16,128]{3,2,1,0:T(8,128)} %param.14) | copy-start | bytes 3145732
  32.0 3.5 %copy-start.18 = (f32[8,16,16]{2,1,0:T(8,128)S(1)}, f32[8,16,16]{2,1,0:T(8,128)}, u32[]{:S(2)}) copy-start(f32[8,16,16]{2,1,0:T(8,128)} %get-tuple-element.134) | copy-start | bytes 24580
  32.0 3.5 %copy-start.23 = (f32[128,128]{1,0:T(8,128)S(1)}, f32[128,128]{1,0:T(8,128)}, u32[]{:S(2)}) copy-start(f32[128,128]{1,0:T(8,128)} %param.16) | copy-start | bytes 196612
  44.6 6.9 %collective-permute-start = (f32[16,16,32]{2,1,0:T(8,128)}, f32[16,16,32]{2,1,0:T(8,128)}, u32[]{:S(2)}, u32[]{:S(2)}) collective-permute-start(f32[16,16,32]{2,1,0:T(8,128)} %multiply_add_fusion.24), channel_id=1, source_target_pairs={{0,8},{8,16},{16,24},{1,9},{9,17},{17,25},{2,10},{10,18},{18,26},{... | collective-permute-start | bytes 98312 | tf_op jit(solution)/shard_map/while/body/eval_jaxpr/ppermute | solution.py:29
  54.8 7.0 %collective-permute-start = (f32[16,16,32]{2,1,0:T(8,128)}, f32[16,16,32]{2,1,0:T(8,128)}, u32[]{:S(2)}, u32[]{:S(2)}) collective-permute-start(f32[16,16,32]{2,1,0:T(8,128)} %multiply_add_fusion.24), channel_id=1, source_target_pairs={{0,8},{8,16},{16,24},{1,9},{9,17},{17,25},{2,10},{10,18},{18,26},{... | collective-permute-start | bytes 98312 | tf_op jit(solution)/shard_map/while/body/eval_jaxpr/ppermute | solution.py:29
  65.0 6.0 %collective-permute-start = (f32[16,16,32]{2,1,0:T(8,128)}, f32[16,16,32]{2,1,0:T(8,128)}, u32[]{:S(2)}, u32[]{:S(2)}) collective-permute-start(f32[16,16,32]{2,1,0:T(8,128)} %multiply_add_fusion.24), channel_id=1, source_target_pairs={{0,8},{8,16},{16,24},{1,9},{9,17},{17,25},{2,10},{10,18},{18,26},{... | collective-permute-start | bytes 98312 | tf_op jit(solution)/shard_map/while/body/eval_jaxpr/ppermute | solution.py:29
  76.9 3.3 %collective-permute-start.6 = (f32[8,1,16,128]{3,2,1,0:T(8,128)S(1)}, f32[8,1,16,128]{3,2,1,0:T(8,128)S(1)}, u32[]{:S(2)}, u32[]{:S(2)}) collective-permute-start(f32[8,1,16,128]{3,2,1,0:T(8,128)S(1)} %get-tuple-element.112), channel_id=1, source_target_pairs={{0,4},{1,5},{2,6},{3,7},{8,12},{9,13},{10,14},{11,15},{16,20},{17,... | collective-permute-start | bytes 196616 | tf_op jit(solution)/shard_map/ppermute | solution.py:17
  78.2 5.0 %collective-permute-start.7 = (f32[8,1,16,128]{3,2,1,0:T(8,128)S(1)}, f32[8,1,16,128]{3,2,1,0:T(8,128)S(1)}, u32[]{:S(2)}, u32[]{:S(2)}) collective-permute-start(f32[8,1,16,128]{3,2,1,0:T(8,128)S(1)} %get-tuple-element.111), channel_id=1, source_target_pairs={{4,0},{5,1},{6,2},{7,3},{12,8},{13,9},{14,10},{15,11},{20,16},{21,... | collective-permute-start | bytes 196616 | tf_op jit(solution)/shard_map/ppermute | solution.py:19
  80.2 12.6 %copy-start.16 = (f32[4,128,32]{1,2,0:T(8,128)S(1)}, f32[4,128,32]{1,2,0:T(8,128)}, u32[]{:S(2)}) copy-start(f32[4,128,32]{1,2,0:T(8,128)} %param.18) | copy-start | bytes 196612
  83.6 12.7 %collective-permute-start.9 = (f32[8,18,1,128]{3,2,1,0:T(1,128)S(1)}, f32[8,18,1,128]{3,2,1,0:T(1,128)S(1)}, u32[]{:S(2)}, u32[]{:S(2)}) collective-permute-start(f32[8,18,1,128]{3,2,1,0:T(1,128)S(1)} %get-tuple-element.109), channel_id=1, source_target_pairs={{1,0},{2,1},{3,2},{5,4},{6,5},{7,6},{9,8},{10,9},{11,10},{13,12},{... | collective-permute-start | bytes 221192 | tf_op jit(solution)/shard_map/ppermute | solution.py:19
  88.8 5.0 %copy-start.11 = (f32[8,16,16]{2,1,0:T(8,128)S(1)}, f32[8,16,16]{2,1,0:T(8,128)}, u32[]{:S(2)}) copy-start(f32[8,16,16]{2,1,0:T(8,128)} %copy-done.10) | copy-start | bytes 24580
  88.9 8.6 %collective-permute-start.8 = (f32[8,18,1,128]{3,2,1,0:T(1,128)S(1)}, f32[8,18,1,128]{3,2,1,0:T(1,128)S(1)}, u32[]{:S(2)}, u32[]{:S(2)}) collective-permute-start(f32[8,18,1,128]{3,2,1,0:T(1,128)S(1)} %get-tuple-element.110), channel_id=1, source_target_pairs={{0,1},{1,2},{2,3},{4,5},{5,6},{6,7},{8,9},{9,10},{10,11},{12,13},{... | collective-permute-start | bytes 221192 | tf_op jit(solution)/shard_map/ppermute | solution.py:17
  100.1 5.2 %copy-start.9 = (f32[8,16,16,128]{3,2,1,0:T(8,128)S(1)}, f32[8,16,16,128]{3,2,1,0:T(8,128)}, u32[]{:S(2)}) copy-start(f32[8,16,16,128]{3,2,1,0:T(8,128)} %param.14) | copy-start | bytes 3145732
  105.3 3.5 %copy-start.19 = (f32[8,16,16]{2,1,0:T(8,128)S(1)}, f32[8,16,16]{2,1,0:T(8,128)}, u32[]{:S(2)}) copy-start(f32[8,16,16]{2,1,0:T(8,128)} %get-tuple-element.134) | copy-start | bytes 24580
  105.3 3.5 %copy-start.24 = (f32[128,128]{1,0:T(8,128)S(1)}, f32[128,128]{1,0:T(8,128)}, u32[]{:S(2)}) copy-start(f32[128,128]{1,0:T(8,128)} %param.16) | copy-start | bytes 196612
  113.8 6.4 %collective-permute-start.1 = (f32[16,16,32]{2,1,0:T(8,128)S(1)}, f32[16,16,32]{2,1,0:T(8,128)S(1)}, u32[]{:S(2)}, u32[]{:S(2)}) collective-permute-start(f32[16,16,32]{2,1,0:T(8,128)S(1)} %multiply_add_fusion.25), channel_id=1, source_target_pairs={{0,8},{8,16},{16,24},{1,9},{9,17},{17,25},{2,10},{10,18},{18,26},{... | collective-permute-start | bytes 98312 | tf_op jit(solution)/shard_map/while/body/eval_jaxpr/ppermute | solution.py:29
  121.9 6.9 %collective-permute-start.1 = (f32[16,16,32]{2,1,0:T(8,128)S(1)}, f32[16,16,32]{2,1,0:T(8,128)S(1)}, u32[]{:S(2)}, u32[]{:S(2)}) collective-permute-start(f32[16,16,32]{2,1,0:T(8,128)S(1)} %multiply_add_fusion.25), channel_id=1, source_target_pairs={{0,8},{8,16},{16,24},{1,9},{9,17},{17,25},{2,10},{10,18},{18,26},{... | collective-permute-start | bytes 98312 | tf_op jit(solution)/shard_map/while/body/eval_jaxpr/ppermute | solution.py:29
  130.6 6.1 %collective-permute-start.1 = (f32[16,16,32]{2,1,0:T(8,128)S(1)}, f32[16,16,32]{2,1,0:T(8,128)S(1)}, u32[]{:S(2)}, u32[]{:S(2)}) collective-permute-start(f32[16,16,32]{2,1,0:T(8,128)S(1)} %multiply_add_fusion.25), channel_id=1, source_target_pairs={{0,8},{8,16},{16,24},{1,9},{9,17},{17,25},{2,10},{10,18},{18,26},{... | collective-permute-start | bytes 98312 | tf_op jit(solution)/shard_map/while/body/eval_jaxpr/ppermute | solution.py:29
  137.3 2.3 %copy-start.3 = (f32[16,16,32]{2,1,0:T(8,128)S(1)}, f32[16,16,32]{2,1,0:T(8,128)}, u32[]{:S(2)}) copy-start(f32[16,16,32]{2,1,0:T(8,128)} %get-tuple-element.70) | copy-start | bytes 98308
  137.3 2.3 %copy-start.7 = (f32[8,16,16,32]{3,2,1,0:T(8,128)S(1)}, f32[8,16,16,32]{3,2,1,0:T(8,128)}, u32[]{:S(2)}) copy-start(f32[8,16,16,32]{3,2,1,0:T(8,128)} %copy-done.6) | copy-start | bytes 786436
  137.3 2.3 %copy-start.12 = (f32[8,16,16]{2,1,0:T(8,128)S(1)}, f32[8,16,16]{2,1,0:T(8,128)}, u32[]{:S(2)}) copy-start(f32[8,16,16]{2,1,0:T(8,128)} %copy-done.10) | copy-start | bytes 24580
  137.3 2.4 %copy-start.21 = (f32[8,32]{1,0:T(8,128)S(1)}, f32[8,32]{1,0:T(8,128)}, u32[]{:S(2)}) copy-start(f32[8,32]{1,0:T(8,128)} %copy-done.20) | copy-start | bytes 3076
  (7 other events, 10.0 us)
where the time goes:
time: 144 us; the launch traced here: 142 us
  waiting for transfers between devices  35.1 us (24%)
  starting transfers between devices  30.9 us (21%)
  other arithmetic  29.7 us (21%)
  matrix products  27.4 us (19%)
  local copies, waits for them, and re-layouts  17.9 us (12%)
    ppermute x6, waiting for transfers between devices, passed_along(): lax.ppermute(value, axis, [(source, source + steps) for source in range(f...  31.7 us
    dot_general x14, matrix products, product(): jnp.einsum('...i,ij->...j', left, right, precision=lax.Precision.HIGHEST,...  27.4 us
    ppermute x4, starting transfers between devices, padded_2(): lax.ppermute(tail, axis, [(i, (i + 1) % count) for i in range(ends)])  12.2 us
    ppermute x4, starting transfers between devices, padded_2(): lax.ppermute(head, axis, [((i + 1) % count, i) for i in range(ends)])  11 us
    concatenate x2, local copies, waits for them, and re-layouts, sweep_once(): jnp.concatenate([scaled * low_y, scaled * high_y, pick_y, scaled * low_z,...  10.4 us
    add x6, other arithmetic, relay_step(): leaving = gain * current + total  7.91 us
    ppermute x6, starting transfers between devices, passed_along(): lax.ppermute(value, axis, [(source, source + steps) for source in range(f...  7.72 us
    select_n x6, other arithmetic, relay_step(): return jnp.where(first, boundary, arrived)  6.75 us
  transfers between devices with their start and end apart: 14, of which 8 were waited for; matrix products, arithmetic and copies ran while one was open for 10% of the time, Pallas kernels for 0%

commit v1 on v0

v1 whole, which is shorter than its diff:
```python
import functools

import jax
import jax.numpy as jnp
from jax import lax
from jax.experimental import pallas as pl
from jax.experimental.pallas import tpu as pltpu
from jax.sharding import PartitionSpec as P

SWEEPS = 2
LANES = 128
WIDTH = 32
OUT = LANES - WIDTH
f32 = jnp.float32
bf16 = jnp.bfloat16


def halves(value):
    high = value.astype(bf16)
    low = (value - high.astype(f32)).astype(bf16)
    return high, low


def doubled(weight):
    row = jnp.concatenate(halves(weight), axis=1)
    return jnp.concatenate([row, row], axis=0)


def product(left, weight):
    wide = jnp.concatenate(halves(left), axis=1)
    both = jnp.dot(wide, weight, preferred_element_type=f32)
    return both[:, :LANES] + both[:, LANES:]


def exact(left, right):
    return jnp.dot(left, right, precision=lax.Precision.HIGHEST, preferred_element_type=f32)


def turned(value, lanes):
    lanes = lanes % LANES
    return value if lanes == 0 else pltpu.roll(value, lanes, 1)


def packed(value, first):
    rows = value.shape[0] // 4
    lane = lax.broadcasted_iota(jnp.int32, (rows, LANES), 1)
    out = None
    for group in range(4):
        piece = turned(value[group * rows : (group + 1) * rows], group * WIDTH - first)
        out = piece if out is None else jnp.where(lane >= group * WIDTH, piece, out)
    return out


def unpacked(value, first):
    return jnp.concatenate([turned(value, first - group * WIDTH) for group in range(4)], axis=0)


def kernel(
    rhs_hbm, guess_hbm, inv_diag, face_mats, extract, lift, transport, boundary, scale, wind,
    out_hbm,
    rhs, guess, traces, scaled_rhs, gain_a, gain_b, mask, through, carried, ahead, base, sums,
    w_extract, w_diag, w_a, w_b, w_lift, w_lift_extract, w_ahead, lift_full, relay_gain, relay_sum,
    start, start_pair, side_out, side_in, relay_out, relay_in,
    load_sem, store_sem, side_send, side_recv, relay_send, relay_recv,
):
    planes, ny, nz, _ = rhs.shape
    cells = ny * nz
    pad = 8
    nz_all = nz + 2 * pad
    place = {axis: lax.axis_index(axis) for axis in ("sweep", "cross", "third")}
    last = {axis: lax.axis_size(axis) - 1 for axis in place}

    guess_copy = pltpu.make_async_copy(guess_hbm, guess, load_sem.at[0])
    rhs_copy = pltpu.make_async_copy(rhs_hbm, rhs, load_sem.at[1])
    guess_copy.start()
    rhs_copy.start()

    barrier = pltpu.get_barrier_semaphore()
    around = []
    for axis in place:
        around.append((axis, 1, place[axis] < last[axis]))
        around.append((axis, -1, place[axis] > 0))
    expected = jnp.int32(0)
    for axis, step, there in around:
        expected = expected + there.astype(jnp.int32)

        @pl.when(there)
        def _(axis=axis, step=step):
            pl.semaphore_signal(
                barrier, inc=1, device_id={axis: place[axis] + step},
                device_id_type=pl.DeviceIdType.MESH,
            )

    faces = ((0, "cross", 1), (1, "cross", -1), (2, "third", 1), (3, "third", -1))

    def has(axis, step):
        return place[axis] < last[axis] if step > 0 else place[axis] > 0

    def side_copy(repeat, face, axis, step):
        return pltpu.make_async_remote_copy(
            src_ref=side_out.at[repeat, face],
            dst_ref=side_in.at[repeat, face],
            send_sem=side_send.at[repeat, face],
            recv_sem=side_recv.at[repeat, face],
            device_id={axis: place[axis] + step},
            device_id_type=pl.DeviceIdType.MESH,
        )

    def relay_copy(repeat):
        return pltpu.make_async_remote_copy(
            src_ref=relay_out.at[repeat],
            dst_ref=relay_in.at[repeat],
            send_sem=relay_send.at[repeat],
            recv_sem=relay_recv.at[repeat],
            device_id={"sweep": place["sweep"] + 1},
            device_id_type=pl.DeviceIdType.MESH,
        )

    lane = lax.broadcasted_iota(jnp.int32, (cells, LANES), 1)
    leaving = lane >= OUT
    flat = traces.reshape(planes * (ny + 2) * nz_all, LANES)

    def rim_rows(plane, z):
        return pl.ds((plane * (ny + 2) + 1) * nz_all + z, ny, stride=nz_all)

    def send_sides(repeat):
        side = [
            jnp.concatenate([traces[p, ny, pad : pad + nz, :] for p in range(planes)], axis=0),
            jnp.concatenate([traces[p, 1, pad : pad + nz, :] for p in range(planes)], axis=0),
            jnp.concatenate([flat[rim_rows(p, pad + nz - 1), :] for p in range(planes)], axis=0),
            jnp.concatenate([flat[rim_rows(p, pad), :] for p in range(planes)], axis=0),
        ]
        for face, axis, step in faces:
            side_out[repeat, face, 0 : side[face].shape[0] // 4, :] = packed(side[face], face * WIDTH)
        for face, axis, step in faces:

            @pl.when(has(axis, step))
            def _(face=face, axis=axis, step=step):
                side_copy(repeat, face, axis, step).start()

    def take_sides(repeat):
        for face, axis, step in faces:

            @pl.when(has(axis, -step))
            def _(face=face, axis=axis, step=step):
                side_copy(repeat, face, axis, step).wait_recv()
                count = planes * (nz if axis == "cross" else ny)
                rows = unpacked(side_in[repeat, face, 0 : count // 4, :], face * WIDTH)
                for p in range(planes):
                    if axis == "cross":
                        piece = rows[p * nz : (p + 1) * nz]
                        traces[p, 0 if step > 0 else ny + 1, pad : pad + nz, :] = piece
                    else:
                        piece = rows[p * ny : (p + 1) * ny]
                        flat[rim_rows(p, pad - 1 if step > 0 else pad + nz), :] = piece

    maps = jnp.concatenate([extract[k] for k in range(4)], axis=1)
    w_extract[...] = doubled(maps)
    traces[:, 0, :, :] = jnp.zeros((planes, nz_all, LANES), f32)
    traces[:, ny + 1, :, :] = jnp.zeros((planes, nz_all, LANES), f32)
    nothing = jnp.zeros((planes, ny, pad, LANES), f32)
    traces[:, 1 : ny + 1, 0:pad, :] = nothing
    traces[:, 1 : ny + 1, pad + nz : nz_all, :] = nothing
    guess_copy.wait()

    def guess_traces(p, _):
        rows = product(guess[p].reshape(cells, LANES), w_extract[...])
        traces[p, 1 : ny + 1, pad : pad + nz, :] = rows.reshape(ny, nz, LANES)
        return 0

    lax.fori_loop(0, planes, guess_traces, 0)
    pl.semaphore_wait(barrier, expected)
    send_sides(0)

    diag = inv_diag[...]
    w_diag[...] = doubled(diag)
    w_a[...] = doubled(exact(jnp.concatenate([face_mats[k] for k in (0, 1, 3, 4)], axis=0), diag))
    w_b[...] = doubled(exact(jnp.concatenate([face_mats[k] for k in (2, 2, 5, 5)], axis=0), diag))
    lift_full[...] = jnp.zeros((LANES, LANES), f32)
    lift_full[OUT:LANES, 0:OUT] = lift[...]
    full = lift_full[...]
    w_lift[...] = doubled(full)
    lift_extract = exact(full, maps)
    w_lift_extract[...] = doubled(lift_extract)
    w_ahead[...] = doubled(
        jnp.concatenate(
            [jnp.zeros((2 * WIDTH, LANES), f32), lift_extract[OUT:LANES], maps[OUT:LANES]], axis=0
        )
    )
    start[...] = jnp.zeros((cells, LANES), f32)
    start[:, 0:WIDTH] = boundary[...].reshape(cells, WIDTH)
    upwind = place["sweep"] == 0
    start[...] = jnp.where(jnp.logical_and(leaving, upwind), turned(start[...], OUT), 0.0)

    unit = (
        lax.broadcasted_iota(jnp.int32, (nz, nz), 0) == lax.broadcasted_iota(jnp.int32, (nz, nz), 1)
    ).astype(f32)
    ones = jnp.ones((nz, LANES), bf16)
    log_rows = jnp.log(jnp.concatenate([transport[...]] * 4, axis=1))
    carried[0] = jnp.where(leaving, 1.0, 0.0)
    ahead_lanes = jnp.logical_and(lane >= OUT - WIDTH, lane < OUT)
    rhs_copy.wait()
    for p in range(planes):
        code = (scale[p] + 4 * wind[0, p] + 8 * wind[1, p]).astype(f32)
        spread = (code[:, None, :] * unit[None]).reshape(cells, nz).astype(bf16)
        code = jnp.dot(spread, ones, preferred_element_type=f32)
        wind_z = code >= 7.5
        code = jnp.where(wind_z, code - 8.0, code)
        wind_y = code >= 3.5
        index = jnp.where(wind_y, code - 4.0, code)
        wind_y = wind_y.astype(f32)
        wind_z = wind_z.astype(f32)
        kappa = 0.5 + 0.25 * index
        inverse = 1.0 / (1.0 + kappa)
        mask[p] = jnp.where(
            lane < WIDTH,
            wind_y,
            jnp.where(lane < 2 * WIDTH, 1.0 - wind_y, jnp.where(lane < OUT, wind_z, 1.0 - wind_z)),
        )
        gain_a[p] = kappa * inverse
        gain_b[p] = inverse
        scaled_rhs[p] = inverse * product(rhs[p].reshape(cells, LANES), w_diag[...])
        factor = jnp.where(leaving, jnp.exp(kappa * log_rows[p : p + 1]), 0.0)
        through[p] = factor
        now = carried[p]
        later = factor * now
        ahead[p] = jnp.where(ahead_lanes, turned(now, -WIDTH), later)
        carried[p + 1] = later
    relay_gain[...] = packed(carried[planes], OUT)

    for repeat in range(SWEEPS):
        final = repeat == SWEEPS - 1
        take_sides(repeat)
        sums[0] = start[...]

        def base_plane(p, _):
            below = traces[p, 0:ny, pad : pad + nz, :].reshape(cells, LANES)
            above = traces[p, 2 : ny + 2, pad : pad + nz, :].reshape(cells, LANES)
            left = traces[p, 1 : ny + 1, pad - 1 : pad - 1 + nz, :].reshape(cells, LANES)
            right = traces[p, 1 : ny + 1, pad + 1 : pad + 1 + nz, :].reshape(cells, LANES)
            near = jnp.where(
                lane < WIDTH,
                below,
                jnp.where(lane < 2 * WIDTH, above, jnp.where(lane < OUT, left, right)),
            )
            by_a = product(near, w_a[...])
            by_b = product(mask[p] * near, w_b[...])
            value = scaled_rhs[p] - gain_a[p] * by_a - gain_b[p] * by_b
            base[p] = value
            sums[p + 1] = through[p] * sums[p] + jnp.where(leaving, value, 0.0)
            return 0

        lax.fori_loop(0, planes, base_plane, 0)
        relay_sum[...] = packed(sums[planes], OUT)

        @pl.when(upwind)
        def _():
            relay_out[repeat] = relay_sum[...]

            @pl.when(last["sweep"] > 0)
            def _():
                relay_copy(repeat).start()

        if not final:

            def local_traces(p, _):
                inner = sums[p]
                value = base[p] + through[p] * inner
                rows = product(value, w_extract[...]) + product(inner, w_lift_extract[...])
                traces[p, 1 : ny + 1, pad : pad + nz, :] = rows.reshape(ny, nz, LANES)
                return 0

            lax.fori_loop(0, planes, local_traces, 0)

        @pl.when(jnp.logical_not(upwind))
        def _():
            relay_copy(repeat).wait_recv()
            arrived = relay_in[repeat]
            relay_out[repeat] = relay_gain[...] * arrived + relay_sum[...]

            @pl.when(place["sweep"] < last["sweep"])
            def _():
                relay_copy(repeat).start()

            here = jnp.where(leaving, unpacked(arrived, OUT), 0.0)
            if final:

                def add_inflow(p, _):
                    sums[p] = sums[p] + carried[p] * here
                    return 0

                lax.fori_loop(0, planes, add_inflow, 0)
            else:
                start_pair[...] = here + turned(here, -WIDTH)

                def add_traces(p, _):
                    rows = product(ahead[p] * start_pair[...], w_ahead[...])
                    traces[p, 1 : ny + 1, pad : pad + nz, :] += rows.reshape(ny, nz, LANES)
                    return 0

                lax.fori_loop(0, planes, add_traces, 0)

        if not final:
            send_sides(repeat + 1)

    for p in range(planes):
        inner = sums[p]
        value = base[p] + through[p] * inner + product(inner, w_lift[...])
        rhs[p] = value.reshape(ny, nz, LANES)
        pltpu.make_async_copy(rhs.at[p], out_hbm.at[p], store_sem.at[p]).start()
    for p in range(planes):
        pltpu.make_async_copy(rhs.at[p], out_hbm.at[p], store_sem.at[p]).wait()

    for repeat in range(SWEEPS):
        for face, axis, step in faces:

            @pl.when(has(axis, step))
            def _(face=face, axis=axis, step=step):
                side_copy(repeat, face, axis, step).wait_send()

        @pl.when(place["sweep"] < last["sweep"])
        def _():
            relay_copy(repeat).wait_send()


def per_device(
    rhs, guess, inv_diag, face_mats, extract, lift, transport, boundary, scale_index, wind
):
    planes, ny, nz, _ = rhs.shape
    cells = ny * nz
    whole = pl.BlockSpec(memory_space=pltpu.VMEM)
    anywhere = pl.BlockSpec(memory_space=pl.ANY)
    field = pltpu.VMEM((planes, ny, nz, LANES), f32)
    rows = pltpu.VMEM((planes, cells, LANES), f32)
    rows_more = pltpu.VMEM((planes + 1, cells, LANES), f32)
    weight = pltpu.VMEM((2 * LANES, 2 * LANES), bf16)
    plane = pltpu.VMEM((cells, LANES), f32)
    relay = pltpu.VMEM((cells // 4, LANES), f32)
    rim = planes * max(ny, nz) // 4
    return pl.pallas_call(
        kernel,
        out_shape=jax.ShapeDtypeStruct(rhs.shape, f32),
        in_specs=[anywhere] * 2 + [whole] * 8,
        out_specs=anywhere,
        scratch_shapes=[
            field, field, pltpu.VMEM((planes, ny + 2, nz + 16, LANES), f32),
            rows, rows, rows, rows, rows, rows_more, rows, rows, rows_more,
            weight, weight, weight, weight, weight, weight, weight,
            pltpu.VMEM((LANES, LANES), f32), relay, relay,
            plane, plane,
            pltpu.VMEM((SWEEPS, 4, rim, LANES), f32),
            pltpu.VMEM((SWEEPS, 4, rim, LANES), f32),
            pltpu.VMEM((SWEEPS, cells // 4, LANES), f32),
            pltpu.VMEM((SWEEPS, cells // 4, LANES), f32),
            pltpu.SemaphoreType.DMA((2,)),
            pltpu.SemaphoreType.DMA((planes,)),
            pltpu.SemaphoreType.DMA((SWEEPS, 4)),
            pltpu.SemaphoreType.DMA((SWEEPS, 4)),
            pltpu.SemaphoreType.DMA((SWEEPS,)),
            pltpu.SemaphoreType.DMA((SWEEPS,)),
        ],
        compiler_params=pltpu.CompilerParams(
            collective_id=0, has_side_effects=True, vmem_limit_bytes=56 * 2**20
        ),
    )(rhs, guess, inv_diag, face_mats, extract, lift, transport, boundary, scale_index, wind)


def solution(mesh):
    return jax.shard_map(
        per_device,
        mesh=mesh,
        in_specs=(
            P("sweep", "cross", "third", None),
            P("sweep", "cross", "third", None),
            P(),
            P(),
            P(),
            P(),
            P("sweep", None),
            P("cross", "third", None),
            P("sweep", "cross", "third"),
            P(None, "sweep", "cross", "third"),
        ),
        out_specs=P("sweep", "cross", "third", None),
        check_vma=False,
    )
```

time: 144 us -> 29.9 us (0.21); the launches traced: 142 us -> 29.6 us
  waiting for transfers between devices: 35.1 us -> 0 us
  starting transfers between devices: 30.9 us -> 0 us
  other arithmetic: 29.7 us -> 0 us
  matrix products: 27.4 us -> 0 us
  Pallas kernels: 0 us -> 25.7 us
  local copies, waits for them, and re-layouts: 17.9 us -> 3.94 us
    ppermute x14 -> x0, waiting for transfers between devices: 35.1 us -> none  [the longest x6 31.7 us: passed_along(): lax.ppermute(value, axis, [(source, source + steps) for source in range(f...]
    ppermute x14 -> x0, starting transfers between devices: 30.9 us -> none  [the longest x4 12.2 us: padded_2(): lax.ppermute(tail, axis, [(i, (i + 1) % count) for i in range(ends)])]
    dot_general x14 -> x0, matrix products: 27.4 us -> none  [product(): jnp.einsum('...i,ij->...j', left, right, precision=lax.Precision.HIGHEST,...]
    pallas_call x0 -> x1, Pallas kernels: none -> 25.7 us  [per_device(): pl.pallas_call(kernel, out_shape=jax.ShapeDtypeStruct(rhs.shape, f32), in...]
    add x11 -> x0, other arithmetic: 13.9 us -> none  [the longest x6 7.91 us: relay_step(): leaving = gain * current + total]
    concatenate x3 -> x0, local copies, waits for them, and re-layouts: 10.4 us -> none  [the longest x2 10.4 us: sweep_once(): jnp.concatenate([scaled * low_y, scaled * high_y, pick_y, scaled * low_z,...]
    select_n x6 -> x0, other arithmetic: 6.75 us -> none  [relay_step(): return jnp.where(first, boundary, arrived)]
    unnamed x16 -> x0, other arithmetic: 4.71 us -> none
  transfers between devices with their start and end apart: 14 -> 0, of which waited for: 8 -> 0; matrix products, arithmetic and copies ran while one was open for 10% -> 0% of each run, Pallas kernels for 0% -> 0%
where the time goes in v1:
time: 29.9 us; the launch traced here: 29.6 us
  Pallas kernels  25.7 us (86%)
  local copies, waits for them, and re-layouts  3.94 us (13%)
    pallas_call x1, Pallas kernels, per_device(): pl.pallas_call(kernel, out_shape=jax.ShapeDtypeStruct(rhs.shape, f32), in...  25.7 us
    unnamed x2, local copies, waits for them, and re-layouts  3.94 us

profile of v1, /device:TPU:25, one launch (start us, length us, event | category | flops | bytes accessed | tf_op | source)
XLA Modules:
  0.0 29.6 jit_solution(16129044920719462484)
XLA Ops:
  0.0 1.7 %copy.11.extract = f32[4,128,32]{2,1,0:T(8,128)} copy(f32[4,128,32]{1,2,0:T(8,128)} %param.14) | data formatting | bytes 131072 | tf_op args[4]
  1.7 25.7 %shard_map.100 = f32[8,16,16,128]{3,2,1,0:T(8,128)} custom-call(f32[8,16,16,128]{3,2,1,0:T(8,128)} %rhs_hbm.1, f32[8,16,16,128]{3,2,1,0:T(8,128)} %guess_hbm.1, f32[128,128]{1,0:T(8,128)} %inv_diag.1, f32[6,32,128]{2,1,0:T(8,128)} %face_mats.1, f32[4,128,32]{2,1,0:T(8,128)} %copy.11.extract, f32[32,96]{1,0:T(8,128)} %lift.1, f32[8,32]{1,0:T(8,128)} %transport.1, ...), custom_call_target="tpu_custom_call" | custom-call | tf_op jit(solution)/shard_map/pallas_call | solution.py:340
  27.4 2.3 %copy.13 = f32[8,16,16,128]{3,2,1,0:T(8,128)} copy(f32[8,16,16,128]{3,2,1,0:T(8,128)} %shard_map.100) | data formatting | bytes 2097152

commit v2 on v1

--- a/solution.py
+++ b/solution.py
@@ -55,14 +55,16 @@
     return jnp.concatenate([turned(value, first - group * WIDTH) for group in range(4)], axis=0)
 
 
-def kernel(
-    rhs_hbm, guess_hbm, inv_diag, face_mats, extract, lift, transport, boundary, scale, wind,
-    out_hbm,
-    rhs, guess, traces, scaled_rhs, gain_a, gain_b, mask, through, carried, ahead, base, sums,
-    w_extract, w_diag, w_a, w_b, w_lift, w_lift_extract, w_ahead, lift_full, relay_gain, relay_sum,
-    start, start_pair, side_out, side_in, relay_out, relay_in,
-    load_sem, store_sem, side_send, side_recv, relay_send, relay_recv,
-):
+def kernel(*refs):
+    sources, out, refs = refs[:10], refs[10], refs[11:]
+    held, refs = refs[:10], refs[10:]
+    rhs, guess, inv_diag, face_mats, extract, lift, transport, boundary, scale, wind = held
+    (
+        traces, scaled_rhs, gain_a, gain_b, mask, through, carried, ahead, base, sums,
+        w_extract, w_diag, w_a, w_b, w_lift, w_lift_extract, w_ahead, lift_full, relay_gain,
+        relay_sum, start, start_pair, side_out, side_in, relay_out, relay_in,
+        load_sem, side_send, side_recv, relay_send, relay_recv,
+    ) = refs
     planes, ny, nz, _ = rhs.shape
     cells = ny * nz
     pad = 8
@@ -70,10 +72,12 @@
     place = {axis: lax.axis_index(axis) for axis in ("sweep", "cross", "third")}
     last = {axis: lax.axis_size(axis) - 1 for axis in place}
 
-    guess_copy = pltpu.make_async_copy(guess_hbm, guess, load_sem.at[0])
-    rhs_copy = pltpu.make_async_copy(rhs_hbm, rhs, load_sem.at[1])
-    guess_copy.start()
-    rhs_copy.start()
+    loads = [
+        pltpu.make_async_copy(source, target, load_sem.at[number])
+        for number, (source, target) in enumerate(zip(sources, held))
+    ]
+    for number in (4, 1, 2, 3, 5, 8, 9, 6, 7, 0):
+        loads[number].start()
 
     barrier = pltpu.get_barrier_semaphore()
     around = []
@@ -154,14 +158,15 @@
                         piece = rows[p * ny : (p + 1) * ny]
                         flat[rim_rows(p, pad - 1 if step > 0 else pad + nz), :] = piece
 
-    maps = jnp.concatenate([extract[k] for k in range(4)], axis=1)
+    loads[4].wait()
+    maps = extract[...].reshape(LANES, LANES).T
     w_extract[...] = doubled(maps)
     traces[:, 0, :, :] = jnp.zeros((planes, nz_all, LANES), f32)
     traces[:, ny + 1, :, :] = jnp.zeros((planes, nz_all, LANES), f32)
     nothing = jnp.zeros((planes, ny, pad, LANES), f32)
     traces[:, 1 : ny + 1, 0:pad, :] = nothing
     traces[:, 1 : ny + 1, pad + nz : nz_all, :] = nothing
-    guess_copy.wait()
+    loads[1].wait()
 
     def guess_traces(p, _):
         rows = product(guess[p].reshape(cells, LANES), w_extract[...])
@@ -172,6 +177,8 @@
     pl.semaphore_wait(barrier, expected)
     send_sides(0)
 
+    for number in (2, 3, 5, 8, 9, 6, 7):
+        loads[number].wait()
     diag = inv_diag[...]
     w_diag[...] = doubled(diag)
     w_a[...] = doubled(exact(jnp.concatenate([face_mats[k] for k in (0, 1, 3, 4)], axis=0), diag))
@@ -199,7 +206,7 @@
     log_rows = jnp.log(jnp.concatenate([transport[...]] * 4, axis=1))
     carried[0] = jnp.where(leaving, 1.0, 0.0)
     ahead_lanes = jnp.logical_and(lane >= OUT - WIDTH, lane < OUT)
-    rhs_copy.wait()
+    loads[0].wait()
     for p in range(planes):
         code = (scale[p] + 4 * wind[0, p] + 8 * wind[1, p]).astype(f32)
         spread = (code[:, None, :] * unit[None]).reshape(cells, nz).astype(bf16)
@@ -306,10 +313,7 @@
     for p in range(planes):
         inner = sums[p]
         value = base[p] + through[p] * inner + product(inner, w_lift[...])
-        rhs[p] = value.reshape(ny, nz, LANES)
-        pltpu.make_async_copy(rhs.at[p], out_hbm.at[p], store_sem.at[p]).start()
-    for p in range(planes):
-        pltpu.make_async_copy(rhs.at[p], out_hbm.at[p], store_sem.at[p]).wait()
+        out[p] = value.reshape(ny, nz, LANES)
 
     for repeat in range(SWEEPS):
         for face, axis, step in faces:
@@ -328,8 +332,9 @@
 ):
     planes, ny, nz, _ = rhs.shape
     cells = ny * nz
+    turned_extract = extract.transpose(0, 2, 1)
     whole = pl.BlockSpec(memory_space=pltpu.VMEM)
-    anywhere = pl.BlockSpec(memory_space=pl.ANY)
+    far = pl.BlockSpec(memory_space=pltpu.HBM)
     field = pltpu.VMEM((planes, ny, nz, LANES), f32)
     rows = pltpu.VMEM((planes, cells, LANES), f32)
     rows_more = pltpu.VMEM((planes + 1, cells, LANES), f32)
@@ -340,10 +345,14 @@
     return pl.pallas_call(
         kernel,
         out_shape=jax.ShapeDtypeStruct(rhs.shape, f32),
-        in_specs=[anywhere] * 2 + [whole] * 8,
-        out_specs=anywhere,
+        in_specs=[far] * 10,
+        out_specs=whole,
         scratch_shapes=[
-            field, field, pltpu.VMEM((planes, ny + 2, nz + 16, LANES), f32),
+            field, field, pltpu.VMEM(inv_diag.shape, f32), pltpu.VMEM(face_mats.shape, f32),
+            pltpu.VMEM(turned_extract.shape, f32), pltpu.VMEM(lift.shape, f32),
+            pltpu.VMEM(transport.shape, f32), pltpu.VMEM(boundary.shape, f32),
+            pltpu.VMEM(scale_index.shape, jnp.int32), pltpu.VMEM(wind.shape, jnp.int32),
+            pltpu.VMEM((planes, ny + 2, nz + 16, LANES), f32),
             rows, rows, rows, rows, rows, rows_more, rows, rows, rows_more,
             weight, weight, weight, weight, weight, weight, weight,
             pltpu.VMEM((LANES, LANES), f32), relay, relay,
@@ -352,17 +361,24 @@
             pltpu.VMEM((SWEEPS, 4, rim, LANES), f32),
             pltpu.VMEM((SWEEPS, cells // 4, LANES), f32),
             pltpu.VMEM((SWEEPS, cells // 4, LANES), f32),
-            pltpu.SemaphoreType.DMA((2,)),
-            pltpu.SemaphoreType.DMA((planes,)),
+            pltpu.SemaphoreType.DMA((10,)),
             pltpu.SemaphoreType.DMA((SWEEPS, 4)),
             pltpu.SemaphoreType.DMA((SWEEPS, 4)),
             pltpu.SemaphoreType.DMA((SWEEPS,)),
             pltpu.SemaphoreType.DMA((SWEEPS,)),
         ],
         compiler_params=pltpu.CompilerParams(
-            collective_id=0, has_side_effects=True, vmem_limit_bytes=56 * 2**20
+            collective_id=0, has_side_effects=True, vmem_limit_bytes=24 * 2**20
         ),
-    )(rhs, guess, inv_diag, face_mats, extract, lift, transport, boundary, scale_index, wind)
+    )(
+        *(
+            pltpu.with_memory_space_constraint(operand, pltpu.HBM)
+            for operand in (
+                rhs, guess, inv_diag, face_mats, turned_extract, lift, transport, boundary,
+                scale_index, wind,
+            )
+        )
+    )
 
 
 def solution(mesh):

time: 29.9 us -> 24.9 us (0.83)
  local copies, waits for them, and re-layouts: 3.94 us -> 0.97 us
  Pallas kernels: 25.7 us -> 23.8 us
    unnamed x2 -> x1, local copies, waits for them, and re-layouts: 3.94 us -> 0.97 us
    pallas_call x1, Pallas kernels: 25.7 us -> 23.8 us  [per_device(): pl.pallas_call(kernel, out_shape=jax.ShapeDtypeStruct(rhs.shape, f32), in...]
where the time goes in v2:
time: 24.9 us; the launch traced here: 24.8 us
  Pallas kernels  23.8 us (96%)
  local copies, waits for them, and re-layouts  0.97 us (4%)
    pallas_call x1, Pallas kernels, per_device(): pl.pallas_call(kernel, out_shape=jax.ShapeDtypeStruct(rhs.shape, f32), in...  23.8 us
    unnamed x1, local copies, waits for them, and re-layouts  0.97 us

profile of v2, /device:TPU:25, one launch (start us, length us, event | category | flops | bytes accessed | tf_op | source)
XLA Modules:
  0.0 24.8 jit_solution(17969119517936598985)
XLA Ops:
  0.0 23.8 %shard_map.100 = f32[8,16,16,128]{3,2,1,0:T(8,128)S(1)} custom-call(f32[8,16,16,128]{3,2,1,0:T(8,128)} %refs_0_.1, f32[8,16,16,128]{3,2,1,0:T(8,128)} %refs_1_.1, f32[128,128]{1,0:T(8,128)} %refs_2_.1, f32[6,32,128]{2,1,0:T(8,128)} %refs_3_.1, f32[4,32,128]{2,1,0:T(8,128)} %bitcast.1, f32[32,96]{1,0:T(8,128)} %refs_5_.1, f32[8,32]{1,0:T(8,128)} %refs_6_.1, ...), custom_call_target="tpu_custom_call" | custom-call | tf_op jit(solution)/shard_map/pallas_call | solution.py:345
  23.8 1.0 %copy.12 = f32[8,16,16,128]{3,2,1,0:T(8,128)} copy(f32[8,16,16,128]{3,2,1,0:T(8,128)S(1)} %shard_map.100) | data formatting | bytes 2097152

commit v3 on v2

--- a/solution.py
+++ b/solution.py
@@ -10,6 +10,7 @@
 SWEEPS = 2
 LANES = 128
 WIDTH = 32
+PIECES = 4
 OUT = LANES - WIDTH
 f32 = jnp.float32
 bf16 = jnp.bfloat16
@@ -110,12 +111,14 @@
             device_id_type=pl.DeviceIdType.MESH,
         )
 
-    def relay_copy(repeat):
+    relay_rows = cells // 4 // PIECES
+
+    def relay_copy(repeat, piece):
         return pltpu.make_async_remote_copy(
-            src_ref=relay_out.at[repeat],
-            dst_ref=relay_in.at[repeat],
-            send_sem=relay_send.at[repeat],
-            recv_sem=relay_recv.at[repeat],
+            src_ref=relay_out.at[repeat, piece],
+            dst_ref=relay_in.at[repeat, piece],
+            send_sem=relay_send.at[repeat, piece],
+            recv_sem=relay_recv.at[repeat, piece],
             device_id={"sweep": place["sweep"] + 1},
             device_id_type=pl.DeviceIdType.MESH,
         )
@@ -173,7 +176,7 @@
         traces[p, 1 : ny + 1, pad : pad + nz, :] = rows.reshape(ny, nz, LANES)
         return 0
 
-    lax.fori_loop(0, planes, guess_traces, 0)
+    lax.fori_loop(0, planes, guess_traces, 0, unroll=4)
     pl.semaphore_wait(barrier, expected)
     send_sides(0)
 
@@ -257,16 +260,19 @@
             sums[p + 1] = through[p] * sums[p] + jnp.where(leaving, value, 0.0)
             return 0
 
-        lax.fori_loop(0, planes, base_plane, 0)
+        lax.fori_loop(0, planes, base_plane, 0, unroll=4)
         relay_sum[...] = packed(sums[planes], OUT)
 
         @pl.when(upwind)
         def _():
-            relay_out[repeat] = relay_sum[...]
-
-            @pl.when(last["sweep"] > 0)
-            def _():
-                relay_copy(repeat).start()
+            for piece in range(PIECES):
+                relay_out[repeat, piece] = relay_sum[
+                    piece * relay_rows : (piece + 1) * relay_rows, :
+                ]
+
+                @pl.when(last["sweep"] > 0)
+                def _(piece=piece):
+                    relay_copy(repeat, piece).start()
 
         if not final:
 
@@ -277,18 +283,22 @@
                 traces[p, 1 : ny + 1, pad : pad + nz, :] = rows.reshape(ny, nz, LANES)
                 return 0
 
-            lax.fori_loop(0, planes, local_traces, 0)
+            lax.fori_loop(0, planes, local_traces, 0, unroll=4)
 
         @pl.when(jnp.logical_not(upwind))
         def _():
-            relay_copy(repeat).wait_recv()
-            arrived = relay_in[repeat]
-            relay_out[repeat] = relay_gain[...] * arrived + relay_sum[...]
-
-            @pl.when(place["sweep"] < last["sweep"])
-            def _():
-                relay_copy(repeat).start()
-
+            for piece in range(PIECES):
+                rows = slice(piece * relay_rows, (piece + 1) * relay_rows)
+                relay_copy(repeat, piece).wait_recv()
+                relay_out[repeat, piece] = (
+                    relay_gain[rows, :] * relay_in[repeat, piece] + relay_sum[rows, :]
+                )
+
+                @pl.when(place["sweep"] < last["sweep"])
+                def _(piece=piece):
+                    relay_copy(repeat, piece).start()
+
+            arrived = jnp.concatenate([relay_in[repeat, piece] for piece in range(PIECES)], axis=0)
             here = jnp.where(leaving, unpacked(arrived, OUT), 0.0)
             if final:
 
@@ -296,7 +306,7 @@
                     sums[p] = sums[p] + carried[p] * here
                     return 0
 
-                lax.fori_loop(0, planes, add_inflow, 0)
+                lax.fori_loop(0, planes, add_inflow, 0, unroll=4)
             else:
                 start_pair[...] = here + turned(here, -WIDTH)
 
@@ -305,7 +315,7 @@
                     traces[p, 1 : ny + 1, pad : pad + nz, :] += rows.reshape(ny, nz, LANES)
                     return 0
 
-                lax.fori_loop(0, planes, add_traces, 0)
+                lax.fori_loop(0, planes, add_traces, 0, unroll=4)
 
         if not final:
             send_sides(repeat + 1)
@@ -324,7 +334,8 @@
 
         @pl.when(place["sweep"] < last["sweep"])
         def _():
-            relay_copy(repeat).wait_send()
+            for piece in range(PIECES):
+                relay_copy(repeat, piece).wait_send()
 
 
 def per_device(
@@ -359,13 +370,13 @@
             plane, plane,
             pltpu.VMEM((SWEEPS, 4, rim, LANES), f32),
             pltpu.VMEM((SWEEPS, 4, rim, LANES), f32),
-            pltpu.VMEM((SWEEPS, cells // 4, LANES), f32),
-            pltpu.VMEM((SWEEPS, cells // 4, LANES), f32),
+            pltpu.VMEM((SWEEPS, PIECES, cells // 4 // PIECES, LANES), f32),
+            pltpu.VMEM((SWEEPS, PIECES, cells // 4 // PIECES, LANES), f32),
             pltpu.SemaphoreType.DMA((10,)),
             pltpu.SemaphoreType.DMA((SWEEPS, 4)),
             pltpu.SemaphoreType.DMA((SWEEPS, 4)),
-            pltpu.SemaphoreType.DMA((SWEEPS,)),
-            pltpu.SemaphoreType.DMA((SWEEPS,)),
+            pltpu.SemaphoreType.DMA((SWEEPS, PIECES)),
+            pltpu.SemaphoreType.DMA((SWEEPS, PIECES)),
         ],
         compiler_params=pltpu.CompilerParams(
             collective_id=0, has_side_effects=True, vmem_limit_bytes=24 * 2**20

time: 24.9 us -> 21.2 us (0.85)
  Pallas kernels: 23.8 us -> 20.1 us
    pallas_call x1, Pallas kernels: 23.8 us -> 20.1 us  [per_device(): pl.pallas_call(kernel, out_shape=jax.ShapeDtypeStruct(rhs.shape, f32), in...]
where the time goes in v3:
time: 21.2 us; the launch traced here: 21.1 us
  Pallas kernels  20.1 us (95%)
  local copies, waits for them, and re-layouts  0.97 us (5%)
    pallas_call x1, Pallas kernels, per_device(): pl.pallas_call(kernel, out_shape=jax.ShapeDtypeStruct(rhs.shape, f32), in...  20.1 us
    unnamed x1, local copies, waits for them, and re-layouts  0.97 us

profile of v3, /device:TPU:25, one launch (start us, length us, event | category | flops | bytes accessed | tf_op | source)
XLA Modules:
  0.0 21.1 jit_solution(17944931275978320994)
XLA Ops:
  0.0 20.1 %shard_map.100 = f32[8,16,16,128]{3,2,1,0:T(8,128)S(1)} custom-call(f32[8,16,16,128]{3,2,1,0:T(8,128)} %refs_0_.1, f32[8,16,16,128]{3,2,1,0:T(8,128)} %refs_1_.1, f32[128,128]{1,0:T(8,128)} %refs_2_.1, f32[6,32,128]{2,1,0:T(8,128)} %refs_3_.1, f32[4,32,128]{2,1,0:T(8,128)} %bitcast.1, f32[32,96]{1,0:T(8,128)} %refs_5_.1, f32[8,32]{1,0:T(8,128)} %refs_6_.1, ...), custom_call_target="tpu_custom_call" | custom-call | tf_op jit(solution)/shard_map/pallas_call | solution.py:356
  20.1 1.0 %copy.12 = f32[8,16,16,128]{3,2,1,0:T(8,128)} copy(f32[8,16,16,128]{3,2,1,0:T(8,128)S(1)} %shard_map.100) | data formatting | bytes 2097152
